TPU v7x, 512 devices: a whole 4x4x16 slice. The times are simulated.
512 devices in a mesh: space: 32 (over y_hi, z), design: 16 (over y_lo, x, core).
Axes of the slice: x: 4, y: 4 (y_hi: 2, y_lo: 2; y = y_hi * 2 + y_lo), z: 16, core: 2. Of those that a mesh axis runs over, the one named last changes fastest.
Arguments:
- states: float32 [16, 5, 128, 32, 128], P('design', None, 'space'), may hold values from -9 to 9
- source: float32 [5, 128, 32, 128], P(None, 'space'), may hold values from -6 to 6
- cell_kind: int32 [128, 32, 16], P('space'), may hold values from 0 to 2
- wall_points: int32 [15, 64], replicated, may hold values from 0 to 16383
- point_shape: float32 [15, 64, 5], replicated, may hold values from -8 to 8
- coupling: float32 [5, 5], replicated, may hold values from -0.45 to 0.45
Outputs:
- advanced: float32 [16, 5, 128, 32, 128], P('design', None, 'space')
Inputs may be any that keep to these rules, and one draw needn't show every extreme that they name: `wall_points`: each value names the wall cell (x, 0, z) as x * 128 + z.
All inputs are finite; a program needn't handle non-finite values.
Results may differ from a plain program's by a relative error of at most 0.0003.
Values sent between devices are 32-bit elements; how exact they have to be, the bound alone decides.
A program may use at most 64 MiB of HBM per device.

v0:
```python
import jax
import jax.numpy as jnp
from jax import lax
from jax.sharding import PartitionSpec as P

ZB = 8
SWEEPS = 4
PSTEPS = 2


def extended(cells, sides, width):
    for axis, dim in sides:
        count = lax.axis_size(axis)
        ends = count - 1
        head = lax.slice_in_dim(cells, 0, width, axis=dim)
        tail = lax.slice_in_dim(cells, cells.shape[dim] - width, cells.shape[dim], axis=dim)
        cells = jnp.concatenate(
            [
                lax.ppermute(tail, axis, [(i, (i + 1) % count) for i in range(ends)]),
                cells,
                lax.ppermute(head, axis, [((i + 1) % count, i) for i in range(ends)]),
            ],
            axis=dim,
        )
    return cells


def spread(value, axis, source):
    kept = jnp.where(lax.axis_index(axis) == source, value, 0).astype(value.dtype)
    return lax.psum(kept, axis)


def kind_term(cell_kind, block_cells):
    kind_cells = jnp.repeat(cell_kind, block_cells, axis=2)
    return (
        0.8
        + 2.2 * (kind_cells == 1).astype(jnp.float32)
        + 0.7 * (kind_cells == 2).astype(jnp.float32)
    )


def coefficient_fields(primal):
    blend = primal[4] - 0.5 * primal[0]
    return jnp.stack([jnp.exp(0.5 * jnp.tanh(blend)) - 1.0, jnp.tanh(primal[1])])


def wall_forcing(points, shapes, first_row, slab_rows, width_y, width_z):
    plane_cells = slab_rows * width_z
    local_index = points - first_row * width_z
    inside = (local_index >= 0) & (local_index < plane_cells)
    slot_index = jnp.where(inside, local_index, plane_cells)
    wall_plane = (
        jnp.zeros((plane_cells, shapes.shape[1]), jnp.float32)
        .at[slot_index]
        .add(shapes, mode="drop")
    )
    wall_plane = jnp.transpose(wall_plane).reshape(shapes.shape[1], slab_rows, 1, width_z)
    return jnp.pad(wall_plane, ((0, 0), (0, 0), (0, width_y - 1), (0, 0)))


def relax(unknowns, target, excess_nu, speed_excess, damping, coupling):
    padded = jnp.pad(unknowns, ((0, 0), (0, 0), (1, 1), (1, 1)))
    conduct = 1.0 + jnp.pad(excess_nu, ((0, 0), (1, 1), (1, 1)))
    centre_nu = conduct[1:-1, 1:-1, 1:-1]
    side_values = [
        conduct[:-2, 1:-1, 1:-1],
        conduct[2:, 1:-1, 1:-1],
        conduct[1:-1, :-2, 1:-1],
        conduct[1:-1, 2:, 1:-1],
        conduct[1:-1, 1:-1, :-2],
        conduct[1:-1, 1:-1, 2:],
    ]
    neighbours = [
        padded[:, :-2, 1:-1, 1:-1],
        padded[:, 2:, 1:-1, 1:-1],
        padded[:, 1:-1, :-2, 1:-1],
        padded[:, 1:-1, 2:, 1:-1],
        padded[:, 1:-1, 1:-1, :-2],
        padded[:, 1:-1, 1:-1, 2:],
    ]
    centre = padded[:, 1:-1, 1:-1, 1:-1]
    upwind = 1.0 + speed_excess
    diagonal = damping + upwind
    offdiag = upwind * neighbours[0]
    for side_nu, near_value in zip(side_values, neighbours):
        face_value = 0.5 * (centre_nu + side_nu)
        diagonal = diagonal + face_value
        offdiag = offdiag + face_value * near_value
    groups = centre.reshape((-1, coupling.shape[0]) + centre.shape[1:])
    coupled = jnp.einsum(
        "fh,ghxyz->gfxyz", coupling, groups, precision=lax.Precision.HIGHEST
    ).reshape(centre.shape)
    return centre + (target + offdiag - diagonal * centre - coupled) / diagonal


def widen(values, with_tile):
    if with_tile:
        return extended(values, (("space", 1),), 1)
    return extended(values, (("space", 1),), 1)


def shards(states, source, cell_kind, wall_points, point_shape, coupling):
    member_state = states[0]
    fields, slab_rows, width_y, width_z = member_state.shape
    member = lax.axis_index("design")
    slab_index = lax.axis_index("space")
    tangent_row = jnp.maximum(member - 1, 0)
    points = lax.dynamic_index_in_dim(wall_points, tangent_row, 0, keepdims=False)
    shapes = lax.dynamic_index_in_dim(point_shape, tangent_row, 0, keepdims=False)
    forcing = wall_forcing(points, shapes, slab_index * slab_rows, slab_rows, width_y, width_z)
    target = jnp.where(member == 0, source, forcing)
    damping = kind_term(cell_kind, ZB)
    unknowns = member_state
    depth = 1
    static = jnp.concatenate([target, damping[None]], axis=0)
    target_wide = static[:-1]
    damping_wide = static[-1]
    count_fields = unknowns.shape[0]
    for pseudo_step in range(PSTEPS):
        local_tile = spread(coefficient_fields(unknowns), "design", 0)
        for group_index in range(SWEEPS // depth):
            if group_index == 0:
                joined = widen(jnp.concatenate([unknowns, local_tile], axis=0), True)
                current = joined[:count_fields]
                coefficient_wide = joined[count_fields:]
            else:
                current = widen(unknowns, False)
            out_rows = slab_rows + 2 * (depth - 1)
            excess_nu = coefficient_wide[0, 0 : out_rows + 2]
            speed_excess = coefficient_wide[1, 1 : 1 + out_rows]
            current = relax(current, target_wide, excess_nu, speed_excess, damping_wide, coupling)
            unknowns = current
    return unknowns[None]


def solution(mesh):
    in_specs = (
        P("design", None, "space", None, None),
        P(None, "space", None, None),
        P("space", None, None),
        P(),
        P(),
        P(),
    )
    out_specs = P("design", None, "space", None, None)
    return jax.shard_map(shards, mesh=mesh, in_specs=in_specs, out_specs=out_specs, check_vma=False)
```

profile of v0, /device:TPU:16, one launch (start us, length us, event | category | flops | bytes accessed | tf_op | source)
XLA Modules:
  0.0 388.6 jit_solution(5971293471004185726)
XLA Ops:
  6.6 1.0 add_bitcast_fusion
  7.6 0.7 maximum_select_fusion
  8.4 0.7 fusion.131
  9.1 0.9 scatter_custom_fusion
  10.1 1.2 copy_select_fusion
  11.4 133.6 %all-reduce.14.cloned.1.call-done = f32[2,4,32,128]{3,2,1,0:T(8,128)} async-done(((f32[2,4,32,128]{3,2,1,0:T(8,128)}), f32[2,4,32,128]{3,2,1,0:T(8,128)}) %all-reduce.14.cloned.1.call-update) | async-done | bytes 131088 | tf_op jit(solution)/shard_map/psum | solution.py:30
  145.0 0.9 pad_maximum_fusion.23
  145.8 3.5 collective-permute-start
  149.3 6.0 %collective-permute-start.1 = (f32[7,1,32,128]{3,2,1,0:T(8,128)S(1)}, f32[7,1,32,128]{3,2,1,0:T(8,128)S(1)}, u32[]{:S(2)}, u32[]{:S(2)}) collective-permute-start(f32[7,1,32,128]{3,2,1,0:T(8,128)S(1)} %get-tuple-element.29), channel_id=1, source_target_pairs={{16,0},{32,16},{48,32},{64,48},{80,64},{96,80},{112,96},{128,112},... | collective-permute-start | bytes 344072 | tf_op jit(solution)/shard_map/ppermute | solution.py:21
  155.4 0.9 collective-permute-done
  156.3 1.4 collective-permute-done.1
  157.6 0.8 maximum_bitcast_fusion
  159.9 1.1 fusion.5
  161.1 1.9 collective-permute-start.2
  163.0 7.9 %collective-permute-start.3 = (f32[5,1,32,128]{3,2,1,0:T(8,128)S(1)}, f32[5,1,32,128]{3,2,1,0:T(8,128)S(1)}, u32[]{:S(2)}, u32[]{:S(2)}) collective-permute-start(f32[5,1,32,128]{3,2,1,0:T(8,128)S(1)} %get-tuple-element.37), channel_id=1, source_target_pairs={{16,0},{32,16},{48,32},{64,48},{80,64},{96,80},{112,96},{128,112},... | collective-permute-start | bytes 245768 | tf_op jit(solution)/shard_map/ppermute | solution.py:21
  171.5 1.5 collective-permute-done.3
  174.2 1.9 collective-permute-start.4
  176.1 7.9 %collective-permute-start.5 = (f32[5,1,32,128]{3,2,1,0:T(8,128)S(1)}, f32[5,1,32,128]{3,2,1,0:T(8,128)S(1)}, u32[]{:S(2)}, u32[]{:S(2)}) collective-permute-start(f32[5,1,32,128]{3,2,1,0:T(8,128)S(1)} %get-tuple-element.35), channel_id=1, source_target_pairs={{16,0},{32,16},{48,32},{64,48},{80,64},{96,80},{112,96},{128,112},... | collective-permute-start | bytes 245768 | tf_op jit(solution)/shard_map/ppermute | solution.py:21
  184.6 1.5 collective-permute-done.5
  187.2 1.9 collective-permute-start.6
  189.2 7.9 %collective-permute-start.7 = (f32[5,1,32,128]{3,2,1,0:T(8,128)S(1)}, f32[5,1,32,128]{3,2,1,0:T(8,128)S(1)}, u32[]{:S(2)}, u32[]{:S(2)}) collective-permute-start(f32[5,1,32,128]{3,2,1,0:T(8,128)S(1)} %get-tuple-element.33), channel_id=1, source_target_pairs={{16,0},{32,16},{48,32},{64,48},{80,64},{96,80},{112,96},{128,112},... | collective-permute-start | bytes 245768 | tf_op jit(solution)/shard_map/ppermute | solution.py:21
  197.1 0.6 fusion.124
  197.7 1.5 collective-permute-done.7
  200.4 0.7 maximum_select_fusion.1
  201.1 122.7 %all-reduce.16.cloned.1.call-done = f32[2,4,32,128]{3,2,1,0:T(8,128)} async-done(((f32[2,4,32,128]{3,2,1,0:T(8,128)}), f32[2,4,32,128]{3,2,1,0:T(8,128)}) %all-reduce.16.cloned.1.call-update) | async-done | bytes 131088 | tf_op jit(solution)/shard_map/psum | solution.py:30
  323.8 1.0 copy.87
  324.8 3.5 collective-permute-start.8
  328.3 6.2 %collective-permute-start.9 = (f32[7,1,32,128]{3,0,2,1:T(8,128)S(1)}, f32[7,1,32,128]{3,0,2,1:T(8,128)S(1)}, u32[]{:S(2)}, u32[]{:S(2)}) collective-permute-start(f32[7,1,32,128]{3,0,2,1:T(8,128)S(1)} %get-tuple-element.18), channel_id=1, source_target_pairs={{16,0},{32,16},{48,32},{64,48},{80,64},{96,80},{112,96},{128,112},... | collective-permute-start | bytes 344072 | tf_op jit(solution)/shard_map/ppermute | solution.py:21
  334.5 1.2 collective-permute-done.8
  335.7 1.2 collective-permute-done.9
  337.2 0.7 select_maximum_fusion.6
  338.1 1.1 fusion.8
  339.2 1.9 collective-permute-start.10
  341.2 8.0 %collective-permute-start.11 = (f32[5,1,32,128]{3,0,2,1:T(8,128)S(1)}, f32[5,1,32,128]{3,0,2,1:T(8,128)S(1)}, u32[]{:S(2)}, u32[]{:S(2)}) collective-permute-start(f32[5,1,32,128]{3,0,2,1:T(8,128)S(1)} %get-tuple-element.24), channel_id=1, source_target_pairs={{16,0},{32,16},{48,32},{64,48},{80,64},{96,80},{112,96},{128,112},... | collective-permute-start | bytes 245768 | tf_op jit(solution)/shard_map/ppermute | solution.py:21
  349.2 1.0 collective-permute-done.10
  350.2 1.5 collective-permute-done.11
  352.2 1.0 fusion.11
  353.2 1.9 collective-permute-start.12
  355.1 8.0 %collective-permute-start.13 = (f32[5,1,32,128]{3,0,2,1:T(8,128)S(1)}, f32[5,1,32,128]{3,0,2,1:T(8,128)S(1)}, u32[]{:S(2)}, u32[]{:S(2)}) collective-permute-start(f32[5,1,32,128]{3,0,2,1:T(8,128)S(1)} %get-tuple-element.22), channel_id=1, source_target_pairs={{16,0},{32,16},{48,32},{64,48},{80,64},{96,80},{112,96},{128,112},... | collective-permute-start | bytes 245768 | tf_op jit(solution)/shard_map/ppermute | solution.py:21
  363.1 1.0 collective-permute-done.12
  364.1 1.5 collective-permute-done.13
  366.1 1.0 fusion.14
  367.1 1.9 collective-permute-start.14
  369.0 8.0 %collective-permute-start.15 = (f32[5,1,32,128]{3,0,2,1:T(8,128)S(1)}, f32[5,1,32,128]{3,0,2,1:T(8,128)S(1)}, u32[]{:S(2)}, u32[]{:S(2)}) collective-permute-start(f32[5,1,32,128]{3,0,2,1:T(8,128)S(1)} %get-tuple-element.20), channel_id=1, source_target_pairs={{16,0},{32,16},{48,32},{64,48},{80,64},{96,80},{112,96},{128,112},... | collective-permute-start | bytes 245768 | tf_op jit(solution)/shard_map/ppermute | solution.py:21
  377.0 1.0 collective-permute-done.14
  378.0 1.5 collective-permute-done.15
  380.0 1.0 fusion.18
  381.0 0.8 copy.89
  (61 shorter events, 8.6 us)
Async XLA Ops:
  6.5 1.8 copy-start
  6.5 138.4 %copy-start.1 = (f32[1,5,4,32,128]{4,3,2,1,0:T(8,128)S(1)}, f32[1,5,4,32,128]{4,3,2,1,0:T(8,128)}, u32[]{:S(2)}) copy-start(f32[1,5,4,32,128]{4,3,2,1,0:T(8,128)} %param.6) | copy-start | bytes 983044
  6.5 4.8 %copy-start.6 = (s32[4,32,16]{1,2,0:T(8,128)S(1)}, s32[4,32,16]{1,2,0:T(8,128)}, u32[]{:S(2)}) copy-start(s32[4,32,16]{1,2,0:T(8,128)} %param.8) | copy-start | bytes 24580
  6.5 138.4 %all-reduce.14.cloned.1.call-start = ((), (), s32[]{:S(2)}) async-start(), calls=%async_computation | async-start | bytes 262144 | tf_op jit(solution)/shard_map/psum | solution.py:30
  8.2 315.5 %all-reduce.16.cloned.1.call-start = ((), (), s32[]{:S(2)}) async-start(), calls=%async_computation.1 | async-start | bytes 262144 | tf_op jit(solution)/shard_map/psum | solution.py:30
  145.0 13.7 %copy-start.2 = (f32[2,4,32,128]{3,2,1,0:T(8,128)S(1)}, f32[2,4,32,128]{3,2,1,0:T(8,128)}, u32[]{:S(2)}) copy-start(f32[2,4,32,128]{3,2,1,0:T(8,128)} %all-reduce.14.cloned.1.call-done) | copy-start | bytes 393220
  145.8 10.5 %collective-permute-start = (f32[7,1,32,128]{3,2,1,0:T(8,128)S(1)}, f32[7,1,32,128]{3,2,1,0:T(8,128)S(1)}, u32[]{:S(2)}, u32[]{:S(2)}) collective-permute-start(f32[7,1,32,128]{3,2,1,0:T(8,128)S(1)} %get-tuple-element.28), channel_id=1, source_target_pairs={{0,16},{16,32},{32,48},{48,64},{64,80},{80,96},{96,112},{112,128},... | collective-permute-start | bytes 344072 | tf_op jit(solution)/shard_map/ppermute | solution.py:19
  149.3 8.3 %collective-permute-start.1 = (f32[7,1,32,128]{3,2,1,0:T(8,128)S(1)}, f32[7,1,32,128]{3,2,1,0:T(8,128)S(1)}, u32[]{:S(2)}, u32[]{:S(2)}) collective-permute-start(f32[7,1,32,128]{3,2,1,0:T(8,128)S(1)} %get-tuple-element.29), channel_id=1, source_target_pairs={{16,0},{32,16},{48,32},{64,48},{80,64},{96,80},{112,96},{128,112},... | collective-permute-start | bytes 344072 | tf_op jit(solution)/shard_map/ppermute | solution.py:21
  159.2 0.7 copy-start.5
  161.1 10.5 %collective-permute-start.2 = (f32[5,1,32,128]{3,2,1,0:T(8,128)S(1)}, f32[5,1,32,128]{3,2,1,0:T(8,128)S(1)}, u32[]{:S(2)}, u32[]{:S(2)}) collective-permute-start(f32[5,1,32,128]{3,2,1,0:T(8,128)S(1)} %get-tuple-element.36), channel_id=1, source_target_pairs={{0,16},{16,32},{32,48},{48,64},{64,80},{80,96},{96,112},{112,128},... | collective-permute-start | bytes 245768 | tf_op jit(solution)/shard_map/ppermute | solution.py:19
  163.0 10.0 %collective-permute-start.3 = (f32[5,1,32,128]{3,2,1,0:T(8,128)S(1)}, f32[5,1,32,128]{3,2,1,0:T(8,128)S(1)}, u32[]{:S(2)}, u32[]{:S(2)}) collective-permute-start(f32[5,1,32,128]{3,2,1,0:T(8,128)S(1)} %get-tuple-element.37), channel_id=1, source_target_pairs={{16,0},{32,16},{48,32},{64,48},{80,64},{96,80},{112,96},{128,112},... | collective-permute-start | bytes 245768 | tf_op jit(solution)/shard_map/ppermute | solution.py:21
  174.2 10.4 %collective-permute-start.4 = (f32[5,1,32,128]{3,2,1,0:T(8,128)S(1)}, f32[5,1,32,128]{3,2,1,0:T(8,128)S(1)}, u32[]{:S(2)}, u32[]{:S(2)}) collective-permute-start(f32[5,1,32,128]{3,2,1,0:T(8,128)S(1)} %get-tuple-element.34), channel_id=1, source_target_pairs={{0,16},{16,32},{32,48},{48,64},{64,80},{80,96},{96,112},{112,128},... | collective-permute-start | bytes 245768 | tf_op jit(solution)/shard_map/ppermute | solution.py:19
  176.1 9.9 %collective-permute-start.5 = (f32[5,1,32,128]{3,2,1,0:T(8,128)S(1)}, f32[5,1,32,128]{3,2,1,0:T(8,128)S(1)}, u32[]{:S(2)}, u32[]{:S(2)}) collective-permute-start(f32[5,1,32,128]{3,2,1,0:T(8,128)S(1)} %get-tuple-element.35), channel_id=1, source_target_pairs={{16,0},{32,16},{48,32},{64,48},{80,64},{96,80},{112,96},{128,112},... | collective-permute-start | bytes 245768 | tf_op jit(solution)/shard_map/ppermute | solution.py:21
  187.2 10.4 %collective-permute-start.6 = (f32[5,1,32,128]{3,2,1,0:T(8,128)S(1)}, f32[5,1,32,128]{3,2,1,0:T(8,128)S(1)}, u32[]{:S(2)}, u32[]{:S(2)}) collective-permute-start(f32[5,1,32,128]{3,2,1,0:T(8,128)S(1)} %get-tuple-element.32), channel_id=1, source_target_pairs={{0,16},{16,32},{32,48},{48,64},{64,80},{80,96},{96,112},{112,128},... | collective-permute-start | bytes 245768 | tf_op jit(solution)/shard_map/ppermute | solution.py:19
  189.2 9.9 %collective-permute-start.7 = (f32[5,1,32,128]{3,2,1,0:T(8,128)S(1)}, f32[5,1,32,128]{3,2,1,0:T(8,128)S(1)}, u32[]{:S(2)}, u32[]{:S(2)}) collective-permute-start(f32[5,1,32,128]{3,2,1,0:T(8,128)S(1)} %get-tuple-element.33), channel_id=1, source_target_pairs={{16,0},{32,16},{48,32},{64,48},{80,64},{96,80},{112,96},{128,112},... | collective-permute-start | bytes 245768 | tf_op jit(solution)/shard_map/ppermute | solution.py:21
  324.8 10.8 %collective-permute-start.8 = (f32[7,1,32,128]{3,0,2,1:T(8,128)S(1)}, f32[7,1,32,128]{3,0,2,1:T(8,128)S(1)}, u32[]{:S(2)}, u32[]{:S(2)}) collective-permute-start(f32[7,1,32,128]{3,0,2,1:T(8,128)S(1)} %get-tuple-element.17), channel_id=1, source_target_pairs={{0,16},{16,32},{32,48},{48,64},{64,80},{80,96},{96,112},{112,128},... | collective-permute-start | bytes 344072 | tf_op jit(solution)/shard_map/ppermute | solution.py:19
  328.3 8.5 %collective-permute-start.9 = (f32[7,1,32,128]{3,0,2,1:T(8,128)S(1)}, f32[7,1,32,128]{3,0,2,1:T(8,128)S(1)}, u32[]{:S(2)}, u32[]{:S(2)}) collective-permute-start(f32[7,1,32,128]{3,0,2,1:T(8,128)S(1)} %get-tuple-element.18), channel_id=1, source_target_pairs={{16,0},{32,16},{48,32},{64,48},{80,64},{96,80},{112,96},{128,112},... | collective-permute-start | bytes 344072 | tf_op jit(solution)/shard_map/ppermute | solution.py:21
  337.0 0.9 copy-start.4
  337.2 1.0 copy-start.3
  339.2 10.9 %collective-permute-start.10 = (f32[5,1,32,128]{3,0,2,1:T(8,128)S(1)}, f32[5,1,32,128]{3,0,2,1:T(8,128)S(1)}, u32[]{:S(2)}, u32[]{:S(2)}) collective-permute-start(f32[5,1,32,128]{3,0,2,1:T(8,128)S(1)} %get-tuple-element.23), channel_id=1, source_target_pairs={{0,16},{16,32},{32,48},{48,64},{64,80},{80,96},{96,112},{112,128},... | collective-permute-start | bytes 245768 | tf_op jit(solution)/shard_map/ppermute | solution.py:19
  341.2 10.5 %collective-permute-start.11 = (f32[5,1,32,128]{3,0,2,1:T(8,128)S(1)}, f32[5,1,32,128]{3,0,2,1:T(8,128)S(1)}, u32[]{:S(2)}, u32[]{:S(2)}) collective-permute-start(f32[5,1,32,128]{3,0,2,1:T(8,128)S(1)} %get-tuple-element.24), channel_id=1, source_target_pairs={{16,0},{32,16},{48,32},{64,48},{80,64},{96,80},{112,96},{128,112},... | collective-permute-start | bytes 245768 | tf_op jit(solution)/shard_map/ppermute | solution.py:21
  353.2 10.9 %collective-permute-start.12 = (f32[5,1,32,128]{3,0,2,1:T(8,128)S(1)}, f32[5,1,32,128]{3,0,2,1:T(8,128)S(1)}, u32[]{:S(2)}, u32[]{:S(2)}) collective-permute-start(f32[5,1,32,128]{3,0,2,1:T(8,128)S(1)} %get-tuple-element.21), channel_id=1, source_target_pairs={{0,16},{16,32},{32,48},{48,64},{64,80},{80,96},{96,112},{112,128},... | collective-permute-start | bytes 245768 | tf_op jit(solution)/shard_map/ppermute | solution.py:19
  355.1 10.5 %collective-permute-start.13 = (f32[5,1,32,128]{3,0,2,1:T(8,128)S(1)}, f32[5,1,32,128]{3,0,2,1:T(8,128)S(1)}, u32[]{:S(2)}, u32[]{:S(2)}) collective-permute-start(f32[5,1,32,128]{3,0,2,1:T(8,128)S(1)} %get-tuple-element.22), channel_id=1, source_target_pairs={{16,0},{32,16},{48,32},{64,48},{80,64},{96,80},{112,96},{128,112},... | collective-permute-start | bytes 245768 | tf_op jit(solution)/shard_map/ppermute | solution.py:21
  367.1 10.9 %collective-permute-start.14 = (f32[5,1,32,128]{3,0,2,1:T(8,128)S(1)}, f32[5,1,32,128]{3,0,2,1:T(8,128)S(1)}, u32[]{:S(2)}, u32[]{:S(2)}) collective-permute-start(f32[5,1,32,128]{3,0,2,1:T(8,128)S(1)} %get-tuple-element.19), channel_id=1, source_target_pairs={{0,16},{16,32},{32,48},{48,64},{64,80},{80,96},{96,112},{112,128},... | collective-permute-start | bytes 245768 | tf_op jit(solution)/shard_map/ppermute | solution.py:19
  369.0 10.5 %collective-permute-start.15 = (f32[5,1,32,128]{3,0,2,1:T(8,128)S(1)}, f32[5,1,32,128]{3,0,2,1:T(8,128)S(1)}, u32[]{:S(2)}, u32[]{:S(2)}) collective-permute-start(f32[5,1,32,128]{3,0,2,1:T(8,128)S(1)} %get-tuple-element.20), channel_id=1, source_target_pairs={{16,0},{32,16},{48,32},{64,48},{80,64},{96,80},{112,96},{128,112},... | collective-permute-start | bytes 245768 | tf_op jit(solution)/shard_map/ppermute | solution.py:21
Sparse Core Ops, SparseCore 0:
  10.3 134.6 all-reduce.13
  201.2 122.4 all-reduce.15
where the time goes:
time: 389 us
  waiting for transfers between devices  273 us (70%)
  starting transfers between devices  78.4 us (20%)
  other arithmetic  13.9 us (4%)
  between operations  13.9 us (4%)
  matrix products  6.8 us (2%)
    psum x2, waiting for transfers between devices, spread(): return lax.psum(kept, axis)  256 us
    ppermute x8, starting transfers between devices, extended(): lax.ppermute(head, axis, [((i + 1) % count, i) for i in range(ends)])  59.9 us
    ppermute x8, starting transfers between devices, extended(): lax.ppermute(tail, axis, [(i, (i + 1) % count) for i in range(ends)])  18.4 us
    ppermute x8, waiting for transfers between devices, extended(): lax.ppermute(head, axis, [((i + 1) % count, i) for i in range(ends)])  11.4 us
  transfers between devices with their start and end apart: 18, of which 15 were waited for; matrix products, arithmetic and copies ran while one was open for 1% of the time, Pallas kernels for 0%

commit v1 on v0

v1 whole, which is shorter than its diff:
```python
import functools

import jax
import jax.numpy as jnp
from jax import lax
from jax.experimental import pallas as pl
from jax.experimental.pallas import tpu as pltpu
from jax.sharding import PartitionSpec as P

ZB = 8
SWEEPS = 4
PSTEPS = 2
FIELDS = 5
MESH = pl.DeviceIdType.MESH


def kernel(
    slabs, rows,
    u_ref, source_ref, kind_ref, points_ref, shapes_ref, coupling_ref,
    out_ref,
    ext, work, coef, weight, target, damping, kind_left, kind_right,
    u_send, u_recv, side_send, side_recv, coef_side, coef_send, coef_recv,
):
    space = lax.axis_index("space")
    design = lax.axis_index("design")
    width_y, width_z = u_ref.shape[2], u_ref.shape[3]
    wide = 3 * rows
    own = slice(rows, 2 * rows)
    lower = slice(0, rows)
    upper = slice(2 * rows, wide)
    parts = (own, lower, upper)

    core = design % 2
    ring = (design // 2) % 4
    pair = design // 8
    primal = design == 0
    has_left = space > 0
    has_right = space < slabs - 1
    relay = core == 0
    to_partner = relay
    to_pair = relay & (pair == 0)
    to_next = relay & (pair == 0) & (ring < 2)
    children = (
        (to_next, design + 2),
        (primal, design + 6),
        (to_pair, design + 8),
        (to_partner, design + 1),
    )
    last = ring // 3
    parent = core * (design - 1) + (1 - core) * (
        pair * (design - 8) + (1 - pair) * (1 - last) * (design - 2)
    )

    def remote(src, dst, send, recv, where):
        return pltpu.make_async_remote_copy(
            src_ref=src, dst_ref=dst, send_sem=send, recv_sem=recv, device_id=where, device_id_type=MESH
        )

    left = (space - 1, design)
    right = (space + 1, design)

    barrier = pltpu.get_barrier_semaphore()
    partners = [(has_left, left), (has_right, right), (design > 0, (space, parent))]
    partners += [(on, (space, child)) for on, child in children]
    expected = jnp.int32(0)
    for on, where in partners:
        expected = expected + on.astype(jnp.int32)

        @pl.when(on)
        def _(where=where):
            pl.semaphore_signal(barrier, inc=1, device_id=where, device_id_type=MESH)

    pl.semaphore_wait(barrier, expected)

    def u_copies(step):
        src = u_ref if step == 0 else ext.at[step, :, own]
        return (
            remote(src, ext.at[step, :, upper], u_send.at[step, 0], u_recv.at[step, 1], left),
            remote(src, ext.at[step, :, lower], u_send.at[step, 1], u_recv.at[step, 0], right),
        )

    kind_copies = (
        remote(kind_ref, kind_right, side_send.at[0], side_recv.at[1], left),
        remote(kind_ref, kind_left, side_send.at[1], side_recv.at[0], right),
    )
    source_copies = (
        remote(source_ref, target.at[:, upper], side_send.at[2], side_recv.at[3], left),
        remote(source_ref, target.at[:, lower], side_send.at[3], side_recv.at[2], right),
    )

    def coef_side_copies(step):
        src = coef.at[step, :, own]
        return (
            remote(src, coef.at[step, :, upper], coef_side.at[step, 0], coef_recv.at[step, 2], left),
            remote(src, coef.at[step, :, lower], coef_side.at[step, 1], coef_recv.at[step, 1], right),
        )

    def tree_copy(step, child, part):
        where = coef.at[step, :, parts[part]]
        return remote(where, where, coef_send.at[step, child, part], coef_recv.at[step, part], (space, children[child][1]))

    sides = (has_left, has_right)
    part_on = (None, has_left, has_right)

    def on_sides(copies, action, also=None):
        for on, copy in zip(sides, copies):

            @pl.when(on if also is None else on & also)
            def _(copy=copy):
                action(copy)

    def recv_sides(copies, also=None):
        for on, copy in zip(sides, copies[::-1]):

            @pl.when(on if also is None else on & also)
            def _(copy=copy):
                copy.wait_recv()

    def start(copy):
        copy.start()

    def wait_send(copy):
        copy.wait_send()

    def forward(step, part, action):
        for child, (on, _) in enumerate(children):
            here = on if part_on[part] is None else on & part_on[part]

            @pl.when(here)
            def _(child=child):
                action(tree_copy(step, child, part))

    def primal_coefficients(step):
        @pl.when(primal)
        def _():
            def row(r, carry):
                if step == 0:
                    p0, p1, p4 = u_ref[0, r], u_ref[1, r], u_ref[4, r]
                else:
                    p0, p1, p4 = ext[step, 0, rows + r], ext[step, 1, rows + r], ext[step, 4, rows + r]
                coef[step, 0, rows + r] = jnp.exp(0.5 * jnp.tanh(p4 - 0.5 * p0)) - 1.0
                coef[step, 1, rows + r] = jnp.tanh(p1)
                return carry

            lax.fori_loop(0, rows, row, 0)

    def blank(step):
        @pl.when(space == 0)
        def _():
            ext[step, :, lower] = jnp.zeros((FIELDS, rows, width_y, width_z), jnp.float32)
            coef[step, :, lower] = jnp.zeros((2, rows, width_y, width_z), jnp.float32)

        @pl.when(space == slabs - 1)
        def _():
            ext[step, :, upper] = jnp.zeros((FIELDS, rows, width_y, width_z), jnp.float32)
            coef[step, :, upper] = jnp.zeros((2, rows, width_y, width_z), jnp.float32)

    row_y = lax.broadcasted_iota(jnp.int32, (width_y, width_z), 0)
    row_z = lax.broadcasted_iota(jnp.int32, (width_y, width_z), 1)
    first_y, last_y = row_y == 0, row_y == width_y - 1
    first_z, last_z = row_z == 0, row_z == width_z - 1

    def shifts(plane):
        return (
            pltpu.roll(plane, 1, 0),
            pltpu.roll(plane, width_y - 1, 0),
            pltpu.roll(plane, 1, 1),
            pltpu.roll(plane, width_z - 1, 1),
        )

    edges = (first_y, last_y, first_z, last_z)

    def weights(step):
        def row(r, carry):
            centre = 1.0 + coef[step, 0, r]
            below = 0.5 * (centre + 1.0 + coef[step, 0, r - 1])
            above = 0.5 * (centre + 1.0 + coef[step, 0, r + 1])
            upwind = 1.0 + coef[step, 1, r]
            diagonal = damping[r] + upwind + below + above
            grid_row = space * rows + r - rows
            weight[0, r] = jnp.where(grid_row == 0, 0.0, below + upwind)
            weight[1, r] = jnp.where(grid_row == slabs * rows - 1, 0.0, above)
            for k, (near, edge) in enumerate(zip(shifts(centre), edges)):
                face = 0.5 * (centre + jnp.where(edge, 1.0, near))
                diagonal = diagonal + face
                weight[2 + k, r] = jnp.where(edge, 0.0, face)
            weight[6, r] = 1.0 / diagonal
            return carry

        lax.fori_loop(1, wide - 1, row, 0)

    def sweep(src, dst, lo, hi, shift):
        def row(r, carry):
            planes = [src[f, r] for f in range(FIELDS)]
            for f in range(FIELDS):
                total = target[f, r] + weight[0, r] * src[f, r - 1] + weight[1, r] * src[f, r + 1]
                for k, near in enumerate(shifts(planes[f])):
                    total = total + weight[2 + k, r] * near
                for h in range(FIELDS):
                    total = total - coupling_ref[f, h] * planes[h]
                dst[f, r - shift] = total * weight[6, r]
            return carry

        lax.fori_loop(lo, hi, row, 0)

    def spread_kinds(kinds, first):
        blocks = kinds[...].astype(jnp.float32).reshape(rows * width_y, width_z // ZB)
        pick_b = lax.broadcasted_iota(jnp.int32, (width_z // ZB, width_z), 0)
        pick_z = lax.broadcasted_iota(jnp.int32, (width_z // ZB, width_z), 1)
        inside = (pick_z >= pick_b * ZB) & (pick_z < pick_b * ZB + ZB)
        cells = jnp.dot(blocks, inside.astype(jnp.float32), preferred_element_type=jnp.float32)
        value = 0.8 + jnp.where(cells == 1.0, 2.2, 0.0) + jnp.where(cells == 2.0, 0.7, 0.0)
        damping[first : first + rows] = value.reshape(rows, width_y, width_z)

    on_sides(kind_copies, start)
    primal_coefficients(0)
    on_sides(coef_side_copies(0), start, primal)

    @pl.when(primal)
    def _():
        forward(0, 0, start)

    on_sides(u_copies(0), start)
    on_sides(source_copies, start, primal)

    blank(0)
    ext[0, :, own] = u_ref[...]

    @pl.when(primal)
    def _():
        target[:, own] = source_ref[...]

        @pl.when(space == 0)
        def _():
            target[:, lower] = jnp.zeros((FIELDS, rows, width_y, width_z), jnp.float32)

        @pl.when(space == slabs - 1)
        def _():
            target[:, upper] = jnp.zeros((FIELDS, rows, width_y, width_z), jnp.float32)

    @pl.when(design > 0)
    def _():
        def row(r, carry):
            cell = (space * rows + r - rows) * width_z + lax.broadcasted_iota(
                jnp.int32, (width_z, points_ref.shape[1]), 0
            )
            hit = (points_ref[...] == cell).astype(jnp.float32)
            wall = lax.dot_general(
                shapes_ref[...], hit, (((1,), (1,)), ((), ())),
                precision=lax.Precision.HIGHEST, preferred_element_type=jnp.float32,
            )
            for f in range(FIELDS):
                line = jnp.broadcast_to(wall[f : f + 1], (width_y, width_z))
                target[f, r] = jnp.where(first_y, line, 0.0)
            return carry

        lax.fori_loop(0, wide, row, 0)

    spread_kinds(kind_ref, rows)

    for step in range(PSTEPS):
        if step > 0:
            primal_coefficients(step)
            on_sides(coef_side_copies(step), start, primal)

            @pl.when(primal)
            def _():
                forward(step, 0, start)

            on_sides(u_copies(step), start)
            blank(step)

        for part in range(3):
            waits = design > 0 if part == 0 else part_on[part]

            @pl.when(waits)
            def _():
                tree_copy(step, 0, part).wait_recv()

            if part == 0:

                @pl.when(design > 0)
                def _():
                    forward(step, part, start)

            else:
                forward(step, part, start)

        if step == 0:
            recv_sides(kind_copies)

            @pl.when(has_left)
            def _():
                spread_kinds(kind_left, 0)

            @pl.when(has_right)
            def _():
                spread_kinds(kind_right, 2 * rows)

            @pl.when(space == 0)
            def _():
                damping[lower] = jnp.zeros((rows, width_y, width_z), jnp.float32)

            @pl.when(space == slabs - 1)
            def _():
                damping[upper] = jnp.zeros((rows, width_y, width_z), jnp.float32)

        weights(step)
        if step == 0:
            recv_sides(source_copies, primal)
        recv_sides(u_copies(step))

        now = ext.at[step]
        for sweep_index in range(SWEEPS):
            margin = sweep_index + 1
            if sweep_index < SWEEPS - 1:
                later = work.at[sweep_index % 2]
                sweep(now, later, margin, wide - margin, 0)
                now = later
            elif step < PSTEPS - 1:
                sweep(now, ext.at[step + 1], margin, wide - margin, 0)
            else:
                sweep(now, out_ref, margin, wide - margin, rows)

    on_sides(kind_copies, wait_send)
    on_sides(source_copies, wait_send, primal)
    for step in range(PSTEPS):
        on_sides(u_copies(step), wait_send)
        on_sides(coef_side_copies(step), wait_send, primal)
        for part in range(3):
            forward(step, part, wait_send)


def shards(states, source, cell_kind, wall_points, point_shape, coupling):
    member_state = states[0]
    fields, rows, width_y, width_z = member_state.shape
    slabs = lax.axis_size("space")
    tangent_row = jnp.maximum(lax.axis_index("design") - 1, 0)
    points = lax.dynamic_slice_in_dim(wall_points, tangent_row, 1, 0)
    shapes = jnp.transpose(lax.dynamic_index_in_dim(point_shape, tangent_row, 0, keepdims=False))
    shapes = jnp.pad(shapes, ((0, 8 - fields), (0, 0)))
    vmem = pl.BlockSpec(memory_space=pltpu.VMEM)
    wide = 3 * rows
    out = pl.pallas_call(
        functools.partial(kernel, slabs, rows),
        name="sweeps",
        out_shape=jax.ShapeDtypeStruct(member_state.shape, jnp.float32),
        in_specs=[vmem] * 5 + [pl.BlockSpec(memory_space=pltpu.SMEM)],
        out_specs=vmem,
        scratch_shapes=[
            pltpu.VMEM((PSTEPS, fields, wide, width_y, width_z), jnp.float32),
            pltpu.VMEM((2, fields, wide, width_y, width_z), jnp.float32),
            pltpu.VMEM((PSTEPS, 2, wide, width_y, width_z), jnp.float32),
            pltpu.VMEM((7, wide, width_y, width_z), jnp.float32),
            pltpu.VMEM((fields, wide, width_y, width_z), jnp.float32),
            pltpu.VMEM((wide, width_y, width_z), jnp.float32),
            pltpu.VMEM(cell_kind.shape, jnp.int32),
            pltpu.VMEM(cell_kind.shape, jnp.int32),
            pltpu.SemaphoreType.DMA((PSTEPS, 2)),
            pltpu.SemaphoreType.DMA((PSTEPS, 2)),
            pltpu.SemaphoreType.DMA((4,)),
            pltpu.SemaphoreType.DMA((4,)),
            pltpu.SemaphoreType.DMA((PSTEPS, 2)),
            pltpu.SemaphoreType.DMA((PSTEPS, 4, 3)),
            pltpu.SemaphoreType.DMA((PSTEPS, 3)),
        ],
        compiler_params=pltpu.CompilerParams(collective_id=0, has_side_effects=True),
    )(member_state, source, cell_kind, points, shapes, coupling)
    return out[None]


def solution(mesh):
    in_specs = (
        P("design", None, "space", None, None),
        P(None, "space", None, None),
        P("space", None, None),
        P(),
        P(),
        P(),
    )
    out_specs = P("design", None, "space", None, None)
    return jax.shard_map(shards, mesh=mesh, in_specs=in_specs, out_specs=out_specs, check_vma=False)
```

time: 389 us -> 61.4 us (0.16)
  the two profiles are of different devices: /device:TPU:16 before, /device:TPU:29 now
where the time goes in v1:
time: 61.4 us; the launch traced here: 61.2 us
  Pallas kernels  56.9 us (93%)
  local copies, waits for them, and re-layouts  4.29 us (7%)
    pallas_call x1, Pallas kernels, shards(): pl.pallas_call(functools.partial(kernel, slabs, rows), name='sweeps', out...  56.9 us
    unnamed x7, local copies, waits for them, and re-layouts  2.45 us
    dynamic_slice x1, local copies, waits for them, and re-layouts, shards(): points = lax.dynamic_slice_in_dim(wall_points, tangent_row, 1, 0)  1.24 us

profile of v1, /device:TPU:29, one launch (start us, length us, event | category | flops | bytes accessed | tf_op | source)
XLA Modules:
  0.0 61.2 jit_solution(15917044360509629060)
XLA Ops:
  0.0 0.0 copy-start
  0.0 0.0 copy-start.1
  0.0 1.2 %constant_dynamic-slice_fusion.1.points_ref = s32[1,64]{1,0:T(1,128)} fusion(s32[15,64]{1,0:T(8,128)} %param.9, s32[]{:T(128)S(6)} %max.3), kind=kLoop, calls=%fused_computation.2 | loop fusion | bytes 516 | tf_op jit(solution)/shard_map/dynamic_slice | solution.py:339
  1.2 0.0 copy-done
  1.3 0.6 pad.4.shapes_ref
  1.9 0.0 copy-done.1
  1.9 0.7 %copy.9.kind_ref = s32[4,32,16]{2,1,0:T(8,128)} copy(s32[4,32,16]{1,2,0:T(8,128)S(1)} %copy-done.1) | data formatting | bytes 16384 | tf_op args[2]
  2.6 56.9 %sweeps.1 = f32[5,4,32,128]{3,2,1,0:T(8,128)} custom-call(f32[5,4,32,128]{3,2,1,0:T(8,128)} %bitcast.8, f32[5,4,32,128]{3,2,1,0:T(8,128)} %source_ref.1, s32[4,32,16]{2,1,0:T(8,128)} %copy.9.kind_ref, s32[1,64]{1,0:T(1,128)} %constant_dynamic-slice_fusion.1.points_ref, f32[8,64]{1,0:T(8,128)} %pad.4.shapes_ref, f32[5,5]{1,0:T(8,128)} %coupling_ref.1), custom_call_target="tpu_custom_call" | custom-call | tf_op jit(solution)/shard_map/sweeps/pallas_call | solution.py:344
  59.5 1.7 %copy.14 = f32[1,5,4,32,128]{4,3,2,1,0:T(8,128)} copy(f32[1,5,4,32,128]{4,3,2,1,0:T(8,128)} %bitcast.7) | data formatting | bytes 655360
  (2 shorter events, 0.0 us)
Async XLA Ops:
  0.0 1.2 %copy-start = (f32[15,64,5]{1,0,2:T(8,128)S(1)}, f32[15,64,5]{1,0,2:T(8,128)}, u32[]{:S(2)}) copy-start(f32[15,64,5]{1,0,2:T(8,128)} %param.10) | copy-start | bytes 57604
  0.0 1.9 %copy-start.1 = (s32[4,32,16]{1,2,0:T(8,128)S(1)}, s32[4,32,16]{1,2,0:T(8,128)}, u32[]{:S(2)}) copy-start(s32[4,32,16]{1,2,0:T(8,128)} %param.8) | copy-start | bytes 24580

commit v2 on v1

--- a/solution.py
+++ b/solution.py
@@ -204,13 +204,15 @@
         lax.fori_loop(lo, hi, row, 0)
 
     def spread_kinds(kinds, first):
-        blocks = kinds[...].astype(jnp.float32).reshape(rows * width_y, width_z // ZB)
         pick_b = lax.broadcasted_iota(jnp.int32, (width_z // ZB, width_z), 0)
         pick_z = lax.broadcasted_iota(jnp.int32, (width_z // ZB, width_z), 1)
         inside = (pick_z >= pick_b * ZB) & (pick_z < pick_b * ZB + ZB)
-        cells = jnp.dot(blocks, inside.astype(jnp.float32), preferred_element_type=jnp.float32)
-        value = 0.8 + jnp.where(cells == 1.0, 2.2, 0.0) + jnp.where(cells == 2.0, 0.7, 0.0)
-        damping[first : first + rows] = value.reshape(rows, width_y, width_z)
+        for r in range(rows):
+            cells = lax.dot_general(
+                kinds[r].astype(jnp.float32), inside.astype(jnp.float32), (((0,), (0,)), ((), ())),
+                preferred_element_type=jnp.float32,
+            )
+            damping[first + r] = 0.8 + jnp.where(cells == 1.0, 2.2, 0.0) + jnp.where(cells == 2.0, 0.7, 0.0)
 
     on_sides(kind_copies, start)
     primal_coefficients(0)
@@ -240,13 +242,24 @@
 
     @pl.when(design > 0)
     def _():
+        tangents, count = points_ref.shape
+        mine = lax.broadcasted_iota(jnp.int32, (tangents, count), 0) == design - 1
+        points = jnp.sum(jnp.where(mine, points_ref[...], 0), axis=0, keepdims=True)
+        shapes = jnp.concatenate(
+            [
+                jnp.sum(jnp.where(mine, shapes_ref[f], 0.0), axis=0, keepdims=True)
+                for f in range(FIELDS)
+            ],
+            axis=0,
+        )
+
         def row(r, carry):
             cell = (space * rows + r - rows) * width_z + lax.broadcasted_iota(
-                jnp.int32, (width_z, points_ref.shape[1]), 0
+                jnp.int32, (width_z, count), 0
             )
-            hit = (points_ref[...] == cell).astype(jnp.float32)
+            hit = (points == cell).astype(jnp.float32)
             wall = lax.dot_general(
-                shapes_ref[...], hit, (((1,), (1,)), ((), ())),
+                shapes, hit, (((1,), (1,)), ((), ())),
                 precision=lax.Precision.HIGHEST, preferred_element_type=jnp.float32,
             )
             for f in range(FIELDS):
@@ -335,16 +348,14 @@
     member_state = states[0]
     fields, rows, width_y, width_z = member_state.shape
     slabs = lax.axis_size("space")
-    tangent_row = jnp.maximum(lax.axis_index("design") - 1, 0)
-    points = lax.dynamic_slice_in_dim(wall_points, tangent_row, 1, 0)
-    shapes = jnp.transpose(lax.dynamic_index_in_dim(point_shape, tangent_row, 0, keepdims=False))
-    shapes = jnp.pad(shapes, ((0, 8 - fields), (0, 0)))
+    kinds = jnp.transpose(cell_kind, (0, 2, 1))
+    shapes = jnp.transpose(point_shape, (2, 0, 1))
     vmem = pl.BlockSpec(memory_space=pltpu.VMEM)
     wide = 3 * rows
     out = pl.pallas_call(
         functools.partial(kernel, slabs, rows),
         name="sweeps",
-        out_shape=jax.ShapeDtypeStruct(member_state.shape, jnp.float32),
+        out_shape=pltpu.VMEM(member_state.shape, jnp.float32),
         in_specs=[vmem] * 5 + [pl.BlockSpec(memory_space=pltpu.SMEM)],
         out_specs=vmem,
         scratch_shapes=[
@@ -354,8 +365,8 @@
             pltpu.VMEM((7, wide, width_y, width_z), jnp.float32),
             pltpu.VMEM((fields, wide, width_y, width_z), jnp.float32),
             pltpu.VMEM((wide, width_y, width_z), jnp.float32),
-            pltpu.VMEM(cell_kind.shape, jnp.int32),
-            pltpu.VMEM(cell_kind.shape, jnp.int32),
+            pltpu.VMEM(kinds.shape, jnp.int32),
+            pltpu.VMEM(kinds.shape, jnp.int32),
             pltpu.SemaphoreType.DMA((PSTEPS, 2)),
             pltpu.SemaphoreType.DMA((PSTEPS, 2)),
             pltpu.SemaphoreType.DMA((4,)),
@@ -365,7 +376,7 @@
             pltpu.SemaphoreType.DMA((PSTEPS, 3)),
         ],
         compiler_params=pltpu.CompilerParams(collective_id=0, has_side_effects=True),
-    )(member_state, source, cell_kind, points, shapes, coupling)
+    )(member_state, source, kinds, wall_points, shapes, coupling)
     return out[None]
 
 

time: 61.4 us -> 56.3 us (0.917)
  local copies, waits for them, and re-layouts: 4.29 us -> 0.73 us
  Pallas kernels: 56.9 us -> 55.5 us
    unnamed x7 -> x1, local copies, waits for them, and re-layouts: 2.45 us -> 0.73 us
    pallas_call x1, Pallas kernels: 56.9 us -> 55.5 us  [shards(): pl.pallas_call(functools.partial(kernel, slabs, rows), name='sweeps', out...]
    dynamic_slice x2 -> x0, local copies, waits for them, and re-layouts: 1.25 us -> none  [the longest x1 1.24 us: shards(): points = lax.dynamic_slice_in_dim(wall_points, tangent_row, 1, 0)]
where the time goes in v2:
time: 56.3 us; the launch traced here: 56.2 us
  Pallas kernels  55.5 us (99%)
  local copies, waits for them, and re-layouts  0.73 us (1%)
    pallas_call x1, Pallas kernels, shards(): pl.pallas_call(functools.partial(kernel, slabs, rows), name='sweeps', out...  55.5 us

profile of v2, /device:TPU:29, one launch (start us, length us, event | category | flops | bytes accessed | tf_op | source)
XLA Modules:
  0.0 56.2 jit_solution(12740621639024032159)
XLA Ops:
  0.0 55.5 %sweeps.1 = f32[5,4,32,128]{3,2,1,0:T(8,128)S(1)} custom-call(f32[5,4,32,128]{3,2,1,0:T(8,128)} %bitcast.5, f32[5,4,32,128]{3,2,1,0:T(8,128)} %source_ref.1, s32[4,16,32]{2,1,0:T(8,128)} %bitcast.7, s32[15,64]{1,0:T(8,128)} %points_ref.1, f32[5,15,64]{2,1,0:T(8,128)} %bitcast.6, f32[5,5]{1,0:T(8,128)} %coupling_ref.1), custom_call_target="tpu_custom_call" | custom-call | tf_op jit(solution)/shard_map/sweeps/pallas_call | solution.py:355
  55.5 0.7 %copy.8 = f32[1,5,4,32,128]{4,3,2,1,0:T(8,128)} copy(f32[1,5,4,32,128]{4,3,2,1,0:T(8,128)S(1)} %bitcast.4) | data formatting | bytes 655360

commit v3 on v2

--- a/solution.py
+++ b/solution.py
@@ -18,7 +18,7 @@
     slabs, rows,
     u_ref, source_ref, kind_ref, points_ref, shapes_ref, coupling_ref,
     out_ref,
-    ext, work, coef, weight, target, damping, kind_left, kind_right,
+    level, coef, weight, target, damping, kind_left, kind_right,
     u_send, u_recv, side_send, side_recv, coef_side, coef_send, coef_recv,
 ):
     space = lax.axis_index("space")
@@ -28,7 +28,6 @@
     own = slice(rows, 2 * rows)
     lower = slice(0, rows)
     upper = slice(2 * rows, wide)
-    parts = (own, lower, upper)
 
     core = design % 2
     ring = (design // 2) % 4
@@ -72,11 +71,18 @@
 
     pl.semaphore_wait(barrier, expected)
 
-    def u_copies(step):
-        src = u_ref if step == 0 else ext.at[step, :, own]
+    def u_copies(step, k):
+        src, first = (u_ref, 0) if step == 0 else (level.at[step, 0], rows)
+        low, high = k, rows - 1 - k
         return (
-            remote(src, ext.at[step, :, upper], u_send.at[step, 0], u_recv.at[step, 1], left),
-            remote(src, ext.at[step, :, lower], u_send.at[step, 1], u_recv.at[step, 0], right),
+            remote(
+                src.at[:, pl.ds(first + low, 1)], level.at[step, 0, :, pl.ds(2 * rows + low, 1)],
+                u_send.at[step, 0, k], u_recv.at[step, 1, k], left,
+            ),
+            remote(
+                src.at[:, pl.ds(first + high, 1)], level.at[step, 0, :, pl.ds(high, 1)],
+                u_send.at[step, 1, k], u_recv.at[step, 0, k], right,
+            ),
         )
 
     kind_copies = (
@@ -88,19 +94,26 @@
         remote(source_ref, target.at[:, lower], side_send.at[3], side_recv.at[2], right),
     )
 
-    def coef_side_copies(step):
-        src = coef.at[step, :, own]
+    def coef_side_copies(step, k):
+        low, high = k, rows - 1 - k
         return (
-            remote(src, coef.at[step, :, upper], coef_side.at[step, 0], coef_recv.at[step, 2], left),
-            remote(src, coef.at[step, :, lower], coef_side.at[step, 1], coef_recv.at[step, 1], right),
-        )
-
-    def tree_copy(step, child, part):
-        where = coef.at[step, :, parts[part]]
-        return remote(where, where, coef_send.at[step, child, part], coef_recv.at[step, part], (space, children[child][1]))
+            remote(
+                coef.at[step, :, pl.ds(rows + low, 1)], coef.at[step, :, pl.ds(2 * rows + low, 1)],
+                coef_side.at[step, 0, k], coef_recv.at[step, 2 * rows + low], left,
+            ),
+            remote(
+                coef.at[step, :, pl.ds(rows + high, 1)], coef.at[step, :, pl.ds(high, 1)],
+                coef_side.at[step, 1, k], coef_recv.at[step, high], right,
+            ),
+        )
+
+    def tree_copy(step, child, row):
+        where = coef.at[step, :, pl.ds(row, 1)]
+        return remote(
+            where, where, coef_send.at[step, child, row], coef_recv.at[step, row], (space, children[child][1])
+        )
 
     sides = (has_left, has_right)
-    part_on = (None, has_left, has_right)
 
     def on_sides(copies, action, also=None):
         for on, copy in zip(sides, copies):
@@ -122,13 +135,52 @@
     def wait_send(copy):
         copy.wait_send()
 
-    def forward(step, part, action):
+    def forward(step, row, action):
         for child, (on, _) in enumerate(children):
-            here = on if part_on[part] is None else on & part_on[part]
-
-            @pl.when(here)
+
+            @pl.when(on)
             def _(child=child):
-                action(tree_copy(step, child, part))
+                action(tree_copy(step, child, row))
+
+    def each_row(body):
+        def one(k, carry):
+            body(k)
+            return carry
+
+        lax.fori_loop(0, rows, one, 0)
+
+    def side_rows(body):
+        def both(k):
+            @pl.when(has_left)
+            def _():
+                body(rows - 1 - k)
+
+            @pl.when(has_right)
+            def _():
+                body(2 * rows + k)
+
+        each_row(both)
+
+    def leave(step):
+        primal_coefficients(step)
+
+        @pl.when(primal)
+        def _():
+            each_row(lambda k: on_sides(coef_side_copies(step, k), start))
+            each_row(lambda k: forward(step, rows + k, start))
+
+        each_row(lambda k: on_sides(u_copies(step, k), start))
+
+    def relay_coefficients(step):
+        def take(row):
+            tree_copy(step, 0, row).wait_recv()
+            forward(step, row, start)
+
+        @pl.when(design > 0)
+        def _():
+            each_row(lambda k: take(rows + k))
+
+        side_rows(take)
 
     def primal_coefficients(step):
         @pl.when(primal)
@@ -137,7 +189,7 @@
                 if step == 0:
                     p0, p1, p4 = u_ref[0, r], u_ref[1, r], u_ref[4, r]
                 else:
-                    p0, p1, p4 = ext[step, 0, rows + r], ext[step, 1, rows + r], ext[step, 4, rows + r]
+                    p0, p1, p4 = (level[step, 0, f, rows + r] for f in (0, 1, 4))
                 coef[step, 0, rows + r] = jnp.exp(0.5 * jnp.tanh(p4 - 0.5 * p0)) - 1.0
                 coef[step, 1, rows + r] = jnp.tanh(p1)
                 return carry
@@ -147,12 +199,12 @@
     def blank(step):
         @pl.when(space == 0)
         def _():
-            ext[step, :, lower] = jnp.zeros((FIELDS, rows, width_y, width_z), jnp.float32)
+            level[step, 0, :, lower] = jnp.zeros((FIELDS, rows, width_y, width_z), jnp.float32)
             coef[step, :, lower] = jnp.zeros((2, rows, width_y, width_z), jnp.float32)
 
         @pl.when(space == slabs - 1)
         def _():
-            ext[step, :, upper] = jnp.zeros((FIELDS, rows, width_y, width_z), jnp.float32)
+            level[step, 0, :, upper] = jnp.zeros((FIELDS, rows, width_y, width_z), jnp.float32)
             coef[step, :, upper] = jnp.zeros((2, rows, width_y, width_z), jnp.float32)
 
     row_y = lax.broadcasted_iota(jnp.int32, (width_y, width_z), 0)
@@ -189,19 +241,36 @@
 
         lax.fori_loop(1, wide - 1, row, 0)
 
-    def sweep(src, dst, lo, hi, shift):
-        def row(r, carry):
-            planes = [src[f, r] for f in range(FIELDS)]
-            for f in range(FIELDS):
-                total = target[f, r] + weight[0, r] * src[f, r - 1] + weight[1, r] * src[f, r + 1]
-                for k, near in enumerate(shifts(planes[f])):
-                    total = total + weight[2 + k, r] * near
-                for h in range(FIELDS):
-                    total = total - coupling_ref[f, h] * planes[h]
-                dst[f, r - shift] = total * weight[6, r]
+    def relax_row(src, dst, r, shift):
+        planes = [src[f, r] for f in range(FIELDS)]
+        for f in range(FIELDS):
+            total = target[f, r] + weight[0, r] * src[f, r - 1] + weight[1, r] * src[f, r + 1]
+            for k, near in enumerate(shifts(planes[f])):
+                total = total + weight[2 + k, r] * near
+            for h in range(FIELDS):
+                total = total - coupling_ref[f, h] * planes[h]
+            dst[f, r - shift] = total * weight[6, r]
+
+    def sweep_own(step, stage):
+        src, shift = level.at[step, stage - 1], 0
+        if stage < SWEEPS:
+            dst = level.at[step, stage]
+        elif step < PSTEPS - 1:
+            dst = level.at[step + 1, 0]
+        else:
+            dst, shift = out_ref, rows
+
+        each_row(lambda k: relax_row(src, dst, rows + k, shift))
+
+    def sweep_halo(step, k):
+        def one(i, carry):
+            stage, side = 1 + i // 2, i % 2
+            out = k + 1 - stage
+            r = rows - out + side * (rows - 1 + 2 * out)
+            relax_row(level.at[step, stage - 1], level.at[step, stage], r, 0)
             return carry
 
-        lax.fori_loop(lo, hi, row, 0)
+        lax.fori_loop(0, 2 * k, one, 0)
 
     def spread_kinds(kinds, first):
         pick_b = lax.broadcasted_iota(jnp.int32, (width_z // ZB, width_z), 0)
@@ -215,18 +284,11 @@
             damping[first + r] = 0.8 + jnp.where(cells == 1.0, 2.2, 0.0) + jnp.where(cells == 2.0, 0.7, 0.0)
 
     on_sides(kind_copies, start)
-    primal_coefficients(0)
-    on_sides(coef_side_copies(0), start, primal)
-
-    @pl.when(primal)
-    def _():
-        forward(0, 0, start)
-
-    on_sides(u_copies(0), start)
+    leave(0)
     on_sides(source_copies, start, primal)
 
     blank(0)
-    ext[0, :, own] = u_ref[...]
+    level[0, 0, :, own] = u_ref[...]
 
     @pl.when(primal)
     def _():
@@ -273,31 +335,10 @@
 
     for step in range(PSTEPS):
         if step > 0:
-            primal_coefficients(step)
-            on_sides(coef_side_copies(step), start, primal)
-
-            @pl.when(primal)
-            def _():
-                forward(step, 0, start)
-
-            on_sides(u_copies(step), start)
+            leave(step)
             blank(step)
 
-        for part in range(3):
-            waits = design > 0 if part == 0 else part_on[part]
-
-            @pl.when(waits)
-            def _():
-                tree_copy(step, 0, part).wait_recv()
-
-            if part == 0:
-
-                @pl.when(design > 0)
-                def _():
-                    forward(step, part, start)
-
-            else:
-                forward(step, part, start)
+        relay_coefficients(step)
 
         if step == 0:
             recv_sides(kind_copies)
@@ -321,27 +362,23 @@
         weights(step)
         if step == 0:
             recv_sides(source_copies, primal)
-        recv_sides(u_copies(step))
-
-        now = ext.at[step]
-        for sweep_index in range(SWEEPS):
-            margin = sweep_index + 1
-            if sweep_index < SWEEPS - 1:
-                later = work.at[sweep_index % 2]
-                sweep(now, later, margin, wide - margin, 0)
-                now = later
-            elif step < PSTEPS - 1:
-                sweep(now, ext.at[step + 1], margin, wide - margin, 0)
-            else:
-                sweep(now, out_ref, margin, wide - margin, rows)
+        for k in range(SWEEPS):
+            recv_sides(u_copies(step, k))
+            if k > 0:
+                sweep_halo(step, k)
+            sweep_own(step, k + 1)
 
     on_sides(kind_copies, wait_send)
     on_sides(source_copies, wait_send, primal)
     for step in range(PSTEPS):
-        on_sides(u_copies(step), wait_send)
-        on_sides(coef_side_copies(step), wait_send, primal)
-        for part in range(3):
-            forward(step, part, wait_send)
+        each_row(lambda k: on_sides(u_copies(step, k), wait_send))
+
+        @pl.when(primal)
+        def _():
+            each_row(lambda k: on_sides(coef_side_copies(step, k), wait_send))
+
+        each_row(lambda k: forward(step, rows + k, wait_send))
+        side_rows(lambda row: forward(step, row, wait_send))
 
 
 def shards(states, source, cell_kind, wall_points, point_shape, coupling):
@@ -359,21 +396,20 @@
         in_specs=[vmem] * 5 + [pl.BlockSpec(memory_space=pltpu.SMEM)],
         out_specs=vmem,
         scratch_shapes=[
-            pltpu.VMEM((PSTEPS, fields, wide, width_y, width_z), jnp.float32),
-            pltpu.VMEM((2, fields, wide, width_y, width_z), jnp.float32),
+            pltpu.VMEM((PSTEPS, SWEEPS, fields, wide, width_y, width_z), jnp.float32),
             pltpu.VMEM((PSTEPS, 2, wide, width_y, width_z), jnp.float32),
             pltpu.VMEM((7, wide, width_y, width_z), jnp.float32),
             pltpu.VMEM((fields, wide, width_y, width_z), jnp.float32),
             pltpu.VMEM((wide, width_y, width_z), jnp.float32),
             pltpu.VMEM(kinds.shape, jnp.int32),
             pltpu.VMEM(kinds.shape, jnp.int32),
-            pltpu.SemaphoreType.DMA((PSTEPS, 2)),
-            pltpu.SemaphoreType.DMA((PSTEPS, 2)),
+            pltpu.SemaphoreType.DMA((PSTEPS, 2, rows)),
+            pltpu.SemaphoreType.DMA((PSTEPS, 2, rows)),
             pltpu.SemaphoreType.DMA((4,)),
             pltpu.SemaphoreType.DMA((4,)),
-            pltpu.SemaphoreType.DMA((PSTEPS, 2)),
-            pltpu.SemaphoreType.DMA((PSTEPS, 4, 3)),
-            pltpu.SemaphoreType.DMA((PSTEPS, 3)),
+            pltpu.SemaphoreType.DMA((PSTEPS, 2, rows)),
+            pltpu.SemaphoreType.DMA((PSTEPS, 4, wide)),
+            pltpu.SemaphoreType.DMA((PSTEPS, wide)),
         ],
         compiler_params=pltpu.CompilerParams(collective_id=0, has_side_effects=True),
     )(member_state, source, kinds, wall_points, shapes, coupling)

time: 56.3 us -> 54.4 us (0.966)
  Pallas kernels: 55.5 us -> 53.5 us
    pallas_call x1, Pallas kernels: 55.5 us -> 53.5 us  [shards(): pl.pallas_call(functools.partial(kernel, slabs, rows), name='sweeps', out...]
where the time goes in v3:
time: 54.4 us; the launch traced here: 54.3 us
  Pallas kernels  53.5 us (98%)
  local copies, waits for them, and re-layouts  0.73 us (1%)
    pallas_call x1, Pallas kernels, shards(): pl.pallas_call(functools.partial(kernel, slabs, rows), name='sweeps', out...  53.5 us

profile of v3, /device:TPU:29, one launch (start us, length us, event | category | flops | bytes accessed | tf_op | source)
XLA Modules:
  0.0 54.3 jit_solution(16234673431565444093)
XLA Ops:
  0.0 53.5 %sweeps.1 = f32[5,4,32,128]{3,2,1,0:T(8,128)S(1)} custom-call(f32[5,4,32,128]{3,2,1,0:T(8,128)} %bitcast.5, f32[5,4,32,128]{3,2,1,0:T(8,128)} %source_ref.1, s32[4,16,32]{2,1,0:T(8,128)} %bitcast.7, s32[15,64]{1,0:T(8,128)} %points_ref.1, f32[5,15,64]{2,1,0:T(8,128)} %bitcast.6, f32[5,5]{1,0:T(8,128)} %coupling_ref.1), custom_call_target="tpu_custom_call" | custom-call | tf_op jit(solution)/shard_map/sweeps/pallas_call | solution.py:392
  53.6 0.7 %copy.8 = f32[1,5,4,32,128]{4,3,2,1,0:T(8,128)} copy(f32[1,5,4,32,128]{4,3,2,1,0:T(8,128)S(1)} %bitcast.4) | data formatting | bytes 655360

commit v4 on v3

--- a/solution.py
+++ b/solution.py
@@ -89,10 +89,18 @@
         remote(kind_ref, kind_right, side_send.at[0], side_recv.at[1], left),
         remote(kind_ref, kind_left, side_send.at[1], side_recv.at[0], right),
     )
-    source_copies = (
-        remote(source_ref, target.at[:, upper], side_send.at[2], side_recv.at[3], left),
-        remote(source_ref, target.at[:, lower], side_send.at[3], side_recv.at[2], right),
-    )
+    def source_copies(k):
+        low, high = k, rows - 1 - k
+        return (
+            remote(
+                source_ref.at[:, pl.ds(low, 1)], target.at[:, pl.ds(2 * rows + low, 1)],
+                side_send.at[2 + 2 * k], side_recv.at[3 + 2 * k], left,
+            ),
+            remote(
+                source_ref.at[:, pl.ds(high, 1)], target.at[:, pl.ds(high, 1)],
+                side_send.at[3 + 2 * k], side_recv.at[2 + 2 * k], right,
+            ),
+        )
 
     def coef_side_copies(step, k):
         low, high = k, rows - 1 - k
@@ -171,16 +179,29 @@
 
         each_row(lambda k: on_sides(u_copies(step, k), start))
 
+    root = relay & (pair == 0)
+
+    def take(step, row):
+        tree_copy(step, 0, row).wait_recv()
+        forward(step, row, start)
+
     def relay_coefficients(step):
-        def take(row):
-            tree_copy(step, 0, row).wait_recv()
-            forward(step, row, start)
-
         @pl.when(design > 0)
         def _():
-            each_row(lambda k: take(rows + k))
-
-        side_rows(take)
+            each_row(lambda k: take(step, rows + k))
+
+        @pl.when(root)
+        def _():
+            side_rows(lambda row: take(step, row))
+
+    def late_coefficients(step, k):
+        @pl.when(has_left & (design > 0) & ~root)
+        def _():
+            take(step, rows - 1 - k)
+
+        @pl.when(has_right & (design > 0) & ~root)
+        def _():
+            take(step, 2 * rows + k)
 
     def primal_coefficients(step):
         @pl.when(primal)
@@ -222,24 +243,31 @@
 
     edges = (first_y, last_y, first_z, last_z)
 
-    def weights(step):
-        def row(r, carry):
-            centre = 1.0 + coef[step, 0, r]
-            below = 0.5 * (centre + 1.0 + coef[step, 0, r - 1])
-            above = 0.5 * (centre + 1.0 + coef[step, 0, r + 1])
-            upwind = 1.0 + coef[step, 1, r]
-            diagonal = damping[r] + upwind + below + above
-            grid_row = space * rows + r - rows
-            weight[0, r] = jnp.where(grid_row == 0, 0.0, below + upwind)
-            weight[1, r] = jnp.where(grid_row == slabs * rows - 1, 0.0, above)
-            for k, (near, edge) in enumerate(zip(shifts(centre), edges)):
-                face = 0.5 * (centre + jnp.where(edge, 1.0, near))
-                diagonal = diagonal + face
-                weight[2 + k, r] = jnp.where(edge, 0.0, face)
-            weight[6, r] = 1.0 / diagonal
-            return carry
-
-        lax.fori_loop(1, wide - 1, row, 0)
+    def weight_row(step, r):
+        centre = 1.0 + coef[step, 0, r]
+        below = 0.5 * (centre + 1.0 + coef[step, 0, r - 1])
+        above = 0.5 * (centre + 1.0 + coef[step, 0, r + 1])
+        upwind = 1.0 + coef[step, 1, r]
+        diagonal = damping[r] + upwind + below + above
+        grid_row = space * rows + r - rows
+        weight[0, r] = jnp.where(grid_row == 0, 0.0, below + upwind)
+        weight[1, r] = jnp.where(grid_row == slabs * rows - 1, 0.0, above)
+        for k, (near, edge) in enumerate(zip(shifts(centre), edges)):
+            face = 0.5 * (centre + jnp.where(edge, 1.0, near))
+            diagonal = diagonal + face
+            weight[2 + k, r] = jnp.where(edge, 0.0, face)
+        weight[6, r] = 1.0 / diagonal
+
+    def weights(step, k):
+        if k == 0:
+            each_row(lambda i: weight_row(step, rows + i))
+        else:
+
+            def one(side, carry):
+                weight_row(step, rows - k + side * (rows - 1 + 2 * k))
+                return carry
+
+            lax.fori_loop(0, 2, one, 0)
 
     def relax_row(src, dst, r, shift):
         planes = [src[f, r] for f in range(FIELDS)]
@@ -285,7 +313,8 @@
 
     on_sides(kind_copies, start)
     leave(0)
-    on_sides(source_copies, start, primal)
+    for k in range(SWEEPS - 1):
+        on_sides(source_copies(k), start, primal)
 
     blank(0)
     level[0, 0, :, own] = u_ref[...]
@@ -359,17 +388,19 @@
             def _():
                 damping[upper] = jnp.zeros((rows, width_y, width_z), jnp.float32)
 
-        weights(step)
-        if step == 0:
-            recv_sides(source_copies, primal)
         for k in range(SWEEPS):
+            late_coefficients(step, k)
+            weights(step, k)
             recv_sides(u_copies(step, k))
             if k > 0:
+                if step == 0:
+                    recv_sides(source_copies(k - 1), primal)
                 sweep_halo(step, k)
             sweep_own(step, k + 1)
 
     on_sides(kind_copies, wait_send)
-    on_sides(source_copies, wait_send, primal)
+    for k in range(SWEEPS - 1):
+        on_sides(source_copies(k), wait_send, primal)
     for step in range(PSTEPS):
         each_row(lambda k: on_sides(u_copies(step, k), wait_send))
 
@@ -405,8 +436,8 @@
             pltpu.VMEM(kinds.shape, jnp.int32),
             pltpu.SemaphoreType.DMA((PSTEPS, 2, rows)),
             pltpu.SemaphoreType.DMA((PSTEPS, 2, rows)),
-            pltpu.SemaphoreType.DMA((4,)),
-            pltpu.SemaphoreType.DMA((4,)),
+            pltpu.SemaphoreType.DMA((2 * rows,)),
+            pltpu.SemaphoreType.DMA((2 * rows,)),
             pltpu.SemaphoreType.DMA((PSTEPS, 2, rows)),
             pltpu.SemaphoreType.DMA((PSTEPS, 4, wide)),
             pltpu.SemaphoreType.DMA((PSTEPS, wide)),

time: 54.4 us -> 49.9 us (0.917)
  Pallas kernels: 53.5 us -> 49 us
    pallas_call x1, Pallas kernels: 53.5 us -> 49 us  [shards(): pl.pallas_call(functools.partial(kernel, slabs, rows), name='sweeps', out...]
where the time goes in v4:
time: 49.9 us; the launch traced here: 49.8 us
  Pallas kernels  49 us (98%)
  local copies, waits for them, and re-layouts  0.73 us (1%)
    pallas_call x1, Pallas kernels, shards(): pl.pallas_call(functools.partial(kernel, slabs, rows), name='sweeps', out...  49 us

profile of v4, /device:TPU:29, one launch (start us, length us, event | category | flops | bytes accessed | tf_op | source)
XLA Modules:
  0.0 49.8 jit_solution(5828639420206600416)
XLA Ops:
  0.0 49.0 %sweeps.1 = f32[5,4,32,128]{3,2,1,0:T(8,128)S(1)} custom-call(f32[5,4,32,128]{3,2,1,0:T(8,128)} %bitcast.5, f32[5,4,32,128]{3,2,1,0:T(8,128)} %source_ref.1, s32[4,16,32]{2,1,0:T(8,128)} %bitcast.7, s32[15,64]{1,0:T(8,128)} %points_ref.1, f32[5,15,64]{2,1,0:T(8,128)} %bitcast.6, f32[5,5]{1,0:T(8,128)} %coupling_ref.1), custom_call_target="tpu_custom_call" | custom-call | tf_op jit(solution)/shard_map/sweeps/pallas_call | solution.py:423
  49.0 0.7 %copy.8 = f32[1,5,4,32,128]{4,3,2,1,0:T(8,128)} copy(f32[1,5,4,32,128]{4,3,2,1,0:T(8,128)S(1)} %bitcast.4) | data formatting | bytes 655360

commit v5 on v4

--- a/solution.py
+++ b/solution.py
@@ -102,21 +102,25 @@
             ),
         )
 
-    def coef_side_copies(step, k):
+    def needed(last):
+        return pl.ds(0, 1 if last else 2)
+
+    def coef_side_copies(step, k, last):
         low, high = k, rows - 1 - k
+        kept = needed(last)
         return (
             remote(
-                coef.at[step, :, pl.ds(rows + low, 1)], coef.at[step, :, pl.ds(2 * rows + low, 1)],
+                coef.at[step, kept, pl.ds(rows + low, 1)], coef.at[step, kept, pl.ds(2 * rows + low, 1)],
                 coef_side.at[step, 0, k], coef_recv.at[step, 2 * rows + low], left,
             ),
             remote(
-                coef.at[step, :, pl.ds(rows + high, 1)], coef.at[step, :, pl.ds(high, 1)],
+                coef.at[step, kept, pl.ds(rows + high, 1)], coef.at[step, kept, pl.ds(high, 1)],
                 coef_side.at[step, 1, k], coef_recv.at[step, high], right,
             ),
         )
 
-    def tree_copy(step, child, row):
-        where = coef.at[step, :, pl.ds(row, 1)]
+    def tree_copy(step, child, row, last=False):
+        where = coef.at[step, needed(last), pl.ds(row, 1)]
         return remote(
             where, where, coef_send.at[step, child, row], coef_recv.at[step, row], (space, children[child][1])
         )
@@ -143,12 +147,12 @@
     def wait_send(copy):
         copy.wait_send()
 
-    def forward(step, row, action):
+    def forward(step, row, action, last=False):
         for child, (on, _) in enumerate(children):
 
             @pl.when(on)
             def _(child=child):
-                action(tree_copy(step, child, row))
+                action(tree_copy(step, child, row, last))
 
     def each_row(body):
         def one(k, carry):
@@ -157,51 +161,66 @@
 
         lax.fori_loop(0, rows, one, 0)
 
+    def but_last(body):
+        def one(k, carry):
+            body(k, False)
+            return carry
+
+        lax.fori_loop(0, rows - 1, one, 0)
+        body(rows - 1, True)
+
     def side_rows(body):
-        def both(k):
+        def both(k, last):
             @pl.when(has_left)
             def _():
-                body(rows - 1 - k)
+                body(rows - 1 - k, last)
 
             @pl.when(has_right)
             def _():
-                body(2 * rows + k)
-
-        each_row(both)
+                body(2 * rows + k, last)
+
+        but_last(both)
 
     def leave(step):
         primal_coefficients(step)
 
         @pl.when(primal)
         def _():
-            each_row(lambda k: on_sides(coef_side_copies(step, k), start))
+            but_last(lambda k, last: on_sides(coef_side_copies(step, k, last), start))
             each_row(lambda k: forward(step, rows + k, start))
 
-        each_row(lambda k: on_sides(u_copies(step, k), start))
+        leave_states(step, design != 1)
+
+    def leave_states(step, who):
+        @pl.when(who)
+        def _():
+            each_row(lambda k: on_sides(u_copies(step, k), start))
 
     root = relay & (pair == 0)
 
-    def take(step, row):
-        tree_copy(step, 0, row).wait_recv()
-        forward(step, row, start)
+    def take(step, row, last=False):
+        tree_copy(step, 0, row, last).wait_recv()
+        forward(step, row, start, last)
 
     def relay_coefficients(step):
         @pl.when(design > 0)
         def _():
             each_row(lambda k: take(step, rows + k))
 
+        leave_states(step, design == 1)
+
         @pl.when(root)
         def _():
-            side_rows(lambda row: take(step, row))
+            side_rows(lambda row, last: take(step, row, last))
 
     def late_coefficients(step, k):
         @pl.when(has_left & (design > 0) & ~root)
         def _():
-            take(step, rows - 1 - k)
+            take(step, rows - 1 - k, k == rows - 1)
 
         @pl.when(has_right & (design > 0) & ~root)
         def _():
-            take(step, 2 * rows + k)
+            take(step, 2 * rows + k, k == rows - 1)
 
     def primal_coefficients(step):
         @pl.when(primal)
@@ -406,10 +425,10 @@
 
         @pl.when(primal)
         def _():
-            each_row(lambda k: on_sides(coef_side_copies(step, k), wait_send))
+            but_last(lambda k, last: on_sides(coef_side_copies(step, k, last), wait_send))
 
         each_row(lambda k: forward(step, rows + k, wait_send))
-        side_rows(lambda row: forward(step, row, wait_send))
+        side_rows(lambda row, last: forward(step, row, wait_send, last))
 
 
 def shards(states, source, cell_kind, wall_points, point_shape, coupling):

time: 49.9 us -> 50.6 us (1.014)
  Pallas kernels: 49 us -> 49.7 us
    pallas_call x1, Pallas kernels: 49 us -> 49.7 us  [shards(): pl.pallas_call(functools.partial(kernel, slabs, rows), name='sweeps', out...]
where the time goes in v5:
time: 50.6 us; the launch traced here: 50.4 us
  Pallas kernels  49.7 us (98%)
  local copies, waits for them, and re-layouts  0.73 us (1%)
    pallas_call x1, Pallas kernels, shards(): pl.pallas_call(functools.partial(kernel, slabs, rows), name='sweeps', out...  49.7 us

profile of v5, /device:TPU:29, one launch (start us, length us, event | category | flops | bytes accessed | tf_op | source)
XLA Modules:
  0.0 50.4 jit_solution(16984445688325039878)
XLA Ops:
  0.0 49.7 %sweeps.1 = f32[5,4,32,128]{3,2,1,0:T(8,128)S(1)} custom-call(f32[5,4,32,128]{3,2,1,0:T(8,128)} %bitcast.5, f32[5,4,32,128]{3,2,1,0:T(8,128)} %source_ref.1, s32[4,16,32]{2,1,0:T(8,128)} %bitcast.7, s32[15,64]{1,0:T(8,128)} %points_ref.1, f32[5,15,64]{2,1,0:T(8,128)} %bitcast.6, f32[5,5]{1,0:T(8,128)} %coupling_ref.1), custom_call_target="tpu_custom_call" | custom-call | tf_op jit(solution)/shard_map/sweeps/pallas_call | solution.py:442
  49.7 0.7 %copy.8 = f32[1,5,4,32,128]{4,3,2,1,0:T(8,128)} copy(f32[1,5,4,32,128]{4,3,2,1,0:T(8,128)S(1)} %bitcast.4) | data formatting | bytes 655360

commit v6 on v5

--- a/solution.py
+++ b/solution.py
@@ -189,12 +189,7 @@
             but_last(lambda k, last: on_sides(coef_side_copies(step, k, last), start))
             each_row(lambda k: forward(step, rows + k, start))
 
-        leave_states(step, design != 1)
-
-    def leave_states(step, who):
-        @pl.when(who)
-        def _():
-            each_row(lambda k: on_sides(u_copies(step, k), start))
+        each_row(lambda k: on_sides(u_copies(step, k), start))
 
     root = relay & (pair == 0)
 
@@ -206,8 +201,6 @@
         @pl.when(design > 0)
         def _():
             each_row(lambda k: take(step, rows + k))
-
-        leave_states(step, design == 1)
 
         @pl.when(root)
         def _():

time: 50.6 us -> 49.8 us (0.984)
  Pallas kernels: 49.7 us -> 49 us
    pallas_call x1, Pallas kernels: 49.7 us -> 49 us  [shards(): pl.pallas_call(functools.partial(kernel, slabs, rows), name='sweeps', out...]
where the time goes in v6:
time: 49.8 us; the launch traced here: 49.7 us
  Pallas kernels  49 us (98%)
  local copies, waits for them, and re-layouts  0.73 us (1%)
    pallas_call x1, Pallas kernels, shards(): pl.pallas_call(functools.partial(kernel, slabs, rows), name='sweeps', out...  49 us

profile of v6, /device:TPU:29, one launch (start us, length us, event | category | flops | bytes accessed | tf_op | source)
XLA Modules:
  0.0 49.7 jit_solution(15453786293389380492)
XLA Ops:
  0.0 49.0 %sweeps.1 = f32[5,4,32,128]{3,2,1,0:T(8,128)S(1)} custom-call(f32[5,4,32,128]{3,2,1,0:T(8,128)} %bitcast.5, f32[5,4,32,128]{3,2,1,0:T(8,128)} %source_ref.1, s32[4,16,32]{2,1,0:T(8,128)} %bitcast.7, s32[15,64]{1,0:T(8,128)} %points_ref.1, f32[5,15,64]{2,1,0:T(8,128)} %bitcast.6, f32[5,5]{1,0:T(8,128)} %coupling_ref.1), custom_call_target="tpu_custom_call" | custom-call | tf_op jit(solution)/shard_map/sweeps/pallas_call | solution.py:435
  49.0 0.7 %copy.8 = f32[1,5,4,32,128]{4,3,2,1,0:T(8,128)} copy(f32[1,5,4,32,128]{4,3,2,1,0:T(8,128)S(1)} %bitcast.4) | data formatting | bytes 655360

commit v7 on v4

--- a/solution.py
+++ b/solution.py
@@ -177,7 +177,13 @@
             each_row(lambda k: on_sides(coef_side_copies(step, k), start))
             each_row(lambda k: forward(step, rows + k, start))
 
-        each_row(lambda k: on_sides(u_copies(step, k), start))
+        if step > 0:
+            each_row(lambda k: on_sides(u_copies(step, k), start))
+        else:
+            for k in range(rows):
+                on_sides(u_copies(0, k), start)
+                if k > 0:
+                    on_sides(source_copies(k - 1), start, primal)
 
     root = relay & (pair == 0)
 
@@ -313,8 +319,6 @@
 
     on_sides(kind_copies, start)
     leave(0)
-    for k in range(SWEEPS - 1):
-        on_sides(source_copies(k), start, primal)
 
     blank(0)
     level[0, 0, :, own] = u_ref[...]

time: 49.9 us -> 49.4 us (0.990)
  Pallas kernels: 49 us -> 48.5 us
    pallas_call x1, Pallas kernels: 49 us -> 48.5 us  [shards(): pl.pallas_call(functools.partial(kernel, slabs, rows), name='sweeps', out...]
where the time goes in v7:
time: 49.4 us; the launch traced here: 49.3 us
  Pallas kernels  48.5 us (98%)
  local copies, waits for them, and re-layouts  0.73 us (1%)
    pallas_call x1, Pallas kernels, shards(): pl.pallas_call(functools.partial(kernel, slabs, rows), name='sweeps', out...  48.5 us

profile of v7, /device:TPU:29, one launch (start us, length us, event | category | flops | bytes accessed | tf_op | source)
XLA Modules:
  0.0 49.3 jit_solution(4789546221467054878)
XLA Ops:
  0.0 48.5 %sweeps.1 = f32[5,4,32,128]{3,2,1,0:T(8,128)S(1)} custom-call(f32[5,4,32,128]{3,2,1,0:T(8,128)} %bitcast.5, f32[5,4,32,128]{3,2,1,0:T(8,128)} %source_ref.1, s32[4,16,32]{2,1,0:T(8,128)} %bitcast.7, s32[15,64]{1,0:T(8,128)} %points_ref.1, f32[5,15,64]{2,1,0:T(8,128)} %bitcast.6, f32[5,5]{1,0:T(8,128)} %coupling_ref.1), custom_call_target="tpu_custom_call" | custom-call | tf_op jit(solution)/shard_map/sweeps/pallas_call | solution.py:427
  48.5 0.7 %copy.8 = f32[1,5,4,32,128]{4,3,2,1,0:T(8,128)} copy(f32[1,5,4,32,128]{4,3,2,1,0:T(8,128)S(1)} %bitcast.4) | data formatting | bytes 655360
